TPU v7x, 128 devices: a whole 4x4x4 slice. The times are simulated.
128 devices in a mesh: shot: 32 (over z, y, core), tm: 4 (over x).
Axes of the slice: x: 4, y: 4, z: 4, core: 2. Of those that a mesh axis runs over, the one named last changes fastest.
Arguments:
- signals: bfloat16 [256, 128, 2048], P('tm', 'shot'), may hold values from -0.59765625 to 0.59765625
- aperture: int32 [128, 128, 128], P('shot'), may hold values from 0 to 2047
- counts: int32 [128, 128], P('shot'), may hold values from 97 to 128, as said below
Outputs:
- prediction: float32 [256, 128, 128], P('tm', None, 'shot')
Inputs may be any that keep to these rules, and one draw needn't show every extreme that they name: Slots j >= counts[r, s] of aperture[r, s] are padding and do not enter the prediction. `counts`: in every draw some output trace uses all 128 slots.
All inputs are finite; a program needn't handle non-finite values.
Results may differ from a plain program's by a relative error of at most 0.0003.
Values may be sent and summed in bfloat16 or wider, within the bound.
No kernel may reach another device: no remote copies, remote signals or barrier semaphores. Data moves between devices by JAX's collectives and lax.ppermute only.
A program may use at most 128 MiB of HBM per device.

v0:
```python
import math
import jax
import jax.numpy as jnp
from jax import lax
from jax.sharding import PartitionSpec as P


def spectra_tables(length):
    sample_ids = jnp.arange(length, dtype=jnp.int32)
    freq_ids = jnp.concatenate(
        [jnp.arange(length + 1, dtype=jnp.int32), jnp.arange(1, length, dtype=jnp.int32)]
    )
    phases = sample_ids[:, None] * freq_ids[None, :] % (2 * length)
    angles = phases.astype(jnp.float32) * (math.pi / length)
    columns = jnp.arange(2 * length, dtype=jnp.int32)
    forward = jnp.where(columns[None, :] <= length, jnp.cos(angles), -jnp.sin(angles))
    weights = jnp.where((freq_ids == 0) | (freq_ids == length), 1.0, 2.0) / (2.0 * length)
    inverse = (
        jnp.where(columns[:, None] <= length, jnp.cos(angles.T), -jnp.sin(angles.T))
        * weights[:, None]
    )
    return (forward, inverse)


def spectral_product(spec_a, spec_b, length):
    real_a = spec_a[..., : length + 1]
    imag_a = spec_a[..., length + 1 :]
    real_b = spec_b[..., : length + 1]
    imag_b = spec_b[..., length + 1 :]
    real_part = real_a * real_b
    middle = real_part[..., 1:length] - imag_a * imag_b
    real_part = jnp.concatenate([real_part[..., :1], middle, real_part[..., length:]], axis=-1)
    imag_part = real_a[..., 1:length] * imag_b + imag_a * real_b[..., 1:length]
    return jnp.concatenate([real_part, imag_part], axis=-1)


def predict(first_side, second_side):
    length, count_s, count_r, span_len = first_side.shape
    forward, inverse = spectra_tables(length)
    block_len = count_s
    for candidate in range(count_s, 0, -1):
        if count_s % candidate == 0 and candidate * count_r * span_len >= 512:
            block_len = candidate
    blocks = count_s // block_len

    def one_block(block_idx):
        part_a = lax.dynamic_slice_in_dim(first_side, block_idx * block_len, block_len, 1).astype(
            jnp.float32
        )
        part_b = lax.dynamic_slice_in_dim(second_side, block_idx * block_len, block_len, 1).astype(
            jnp.float32
        )
        spec_a = jnp.einsum("tsrj,tk->srjk", part_a, forward, precision=lax.Precision.HIGHEST)
        spec_b = jnp.einsum("tsrj,tk->srjk", part_b, forward, precision=lax.Precision.HIGHEST)
        return jnp.sum(spectral_product(spec_a, spec_b, length), axis=2)

    spectra = lax.map(one_block, jnp.arange(blocks, dtype=jnp.int32))
    spectra = spectra.reshape(count_s, count_r, 2 * length)
    return jnp.einsum("srk,kt->tsr", spectra, inverse, precision=lax.Precision.HIGHEST)


def convolve(halves):
    return predict(halves[0], halves[1])


def body(signals, aperture, counts):
    length_win, shots_here, stations = signals.shape
    span_len = aperture.shape[2]
    offsets = jnp.arange(shots_here, dtype=jnp.int32) * stations
    gathered_lists = lax.all_to_all(aperture, "shot", split_axis=1, concat_axis=0, tiled=True)
    live_mask = jnp.arange(span_len, dtype=jnp.int32)[None, None, :] < counts[:, :, None]
    live_mask = jnp.transpose(live_mask, (1, 0, 2))
    own_index = jnp.transpose(aperture + offsets[:, None, None], (1, 0, 2))
    sender_index = jnp.transpose(gathered_lists + offsets[None, :, None], (1, 0, 2))
    flat_signals = signals.reshape(length_win, shots_here * stations)
    own_traces = jnp.take(flat_signals, own_index, axis=1)
    local_side = jnp.where(live_mask[None], own_traces, jnp.zeros_like(own_traces))
    remote_side = jnp.take(flat_signals, sender_index, axis=1)
    arrived = lax.all_to_all(remote_side, "shot", split_axis=2, concat_axis=1, tiled=True)
    merged = convolve(
        (
            lax.all_to_all(arrived, "tm", split_axis=1, concat_axis=0, tiled=True),
            lax.all_to_all(local_side, "tm", split_axis=1, concat_axis=0, tiled=True),
        )
    )
    result = lax.all_to_all(merged, "tm", split_axis=0, concat_axis=1, tiled=True)
    return result


def solution(mesh):
    in_specs = (P("tm", "shot", None), P("shot", None, None), P("shot", None))
    out_specs = P("tm", None, "shot")
    return jax.shard_map(body, mesh=mesh, in_specs=in_specs, out_specs=out_specs, check_vma=False)
```

profile of v0, /device:TPU:8, one launch (start us, length us, event | category | flops | bytes accessed | tf_op | source)
XLA Modules:
  0.0 1156.7 jit_solution(7991697897503498598)
XLA Ops:
  1.8 8.5 all-to-all-start
  13.3 4.8 all-to-all-done
  18.3 229.0 %gather_fusion = bf16[65536,64]{1,0:T(8,128)(2,1)} fusion(bf16[64,8192]{0,1:T(8,128)(2,1)S(1)} %bitcast.76, s32[65536]{0:T(1024)S(1)} %broadcast_clamp_fusion.1), kind=kCustom, calls=%fused_computation | custom fusion | bytes 17039360 | tf_op jit(solution)/shard_map/jit(_take)/gather | solution.py:78
  247.3 15.8 %copy.40 = bf16[4,128,128,64]{2,3,0,1:T(8,128)(2,1)} copy(bf16[4,128,128,64]{3,2,1,0:T(8,128)(2,1)} %bitcast.79) | data formatting | bytes 16777216 | tf_op jit(solution)/shard_map/jit(_take)/gather | solution.py:78
  263.3 7.6 select_bitcast_fusion.1
  270.8 6.1 all-to-all-start.1
  277.4 229.0 %gather_fusion.1 = bf16[65536,64]{1,0:T(8,128)(2,1)} fusion(bf16[64,8192]{0,1:T(8,128)(2,1)S(1)} %bitcast.77, s32[65536]{0:T(1024)S(1)} %broadcast_clamp_fusion), kind=kCustom, calls=%fused_computation.1 | custom fusion | bytes 17039360 | tf_op jit(solution)/shard_map/jit(_take)/gather | solution.py:76
  506.4 19.1 %copy.48 = bf16[128,4,128,64]{2,1,3,0:T(4,128)(2,1)} copy(bf16[128,4,128,64]{3,2,1,0:T(8,128)(2,1)} %bitcast.78) | data formatting | bytes 16777216 | tf_op jit(solution)/shard_map/jit(_take)/gather | solution.py:76
  525.9 8.5 select_bitcast_fusion
  534.4 5.6 all-to-all-start.3
  540.0 9.6 copy.42
  549.7 84.8 %all-to-all-done.3 = bf16[64,128,4,128]{3,2,0,1:T(4,128)(2,1)} async-done(((bf16[64,128,4,128]{3,2,0,1:T(4,128)(2,1)}), bf16[64,128,4,128]{3,2,0,1:T(4,128)(2,1)}, u32[]{:S(2)}, u32[]{:S(2)}) %all-to-all-start.3) | async-done | bytes 8388640 | tf_op jit(solution)/shard_map/all_to_all | solution.py:83
  634.4 5.8 all-to-all-start.2
  640.4 16.3 %copy.49 = bf16[64,128,4,128]{3,1,2,0:T(8,128)(2,1)} copy(bf16[64,128,4,128]{3,2,0,1:T(4,128)(2,1)} %all-to-all-done.3) | data formatting | bytes 16777216 | tf_op jit(solution)/shard_map/all_to_all | solution.py:83
  656.7 9.3 copy.50
  665.9 13.7 %copy.52 = bf16[256,32,4,128]{0,3,2,1:T(8,128)(2,1)} copy(bf16[256,32,4,128]{3,1,2,0:T(8,128)(2,1)} %bitcast.82) | data formatting | bytes 16777216
  679.7 53.9 %all-to-all-done.2 = bf16[64,128,4,128]{3,0,2,1:T(8,128)(2,1)} async-done(((bf16[64,128,4,128]{3,0,2,1:T(8,128)(2,1)}), bf16[64,128,4,128]{3,0,2,1:T(8,128)(2,1)}, u32[]{:S(2)}, u32[]{:S(2)}) %all-to-all-start.2) | async-done | bytes 8388640 | tf_op jit(solution)/shard_map/all_to_all | solution.py:82
  733.6 12.0 %copy.44 = bf16[4,64,32,4,128]{4,2,3,1,0:T(8,128)(2,1)} copy(bf16[4,64,32,4,128]{4,1,3,2,0:T(8,128)(2,1)} %bitcast.15) | data formatting | bytes 16777216 | tf_op jit(solution)/shard_map/all_to_all | solution.py:82
  745.7 13.8 %copy.51 = bf16[256,32,4,128]{0,3,2,1:T(8,128)(2,1)} copy(bf16[256,32,4,128]{3,1,2,0:T(8,128)(2,1)} %bitcast.83) | data formatting | bytes 16777216
  759.4 382.9 %while.11 = (s32[]{:T(128)}, f32[32,1,4,512]{3,2,1,0:T(4,128)S(1)}, s32[32]{0:T(128)S(1)}, bf16[256,32,4,128]{0,3,2,1:T(8,128)(2,1)}, bf16[256,32,4,128]{0,3,2,1...) while((s32[]{:T(128)}, f32[32,1,4,512]{3,2,1,0:T(4,128)S(1)}, ...), condition=%wide.region_2.3_spmd.clone, body=%wide.region_0.0_spmd.clone.sunk | while | flops 1616637952 | bytes 8942751 | solution.py:57
  761.9 4.0 convolution_bitcast_fusion.4
  766.0 4.0 convolution_bitcast_fusion.5
  773.9 4.0 convolution_bitcast_fusion.4
  777.9 4.0 convolution_bitcast_fusion.5
  785.9 4.0 convolution_bitcast_fusion.4
  789.9 4.0 convolution_bitcast_fusion.5
  797.8 4.0 convolution_bitcast_fusion.4
  801.8 4.0 convolution_bitcast_fusion.5
  809.8 4.0 convolution_bitcast_fusion.4
  813.8 4.0 convolution_bitcast_fusion.5
  821.7 4.0 convolution_bitcast_fusion.4
  825.7 4.0 convolution_bitcast_fusion.5
  833.7 4.0 convolution_bitcast_fusion.4
  837.7 4.0 convolution_bitcast_fusion.5
  845.6 4.0 convolution_bitcast_fusion.4
  849.7 4.0 convolution_bitcast_fusion.5
  861.6 4.0 convolution_bitcast_fusion.5
  869.6 4.0 convolution_bitcast_fusion.4
  873.6 4.0 convolution_bitcast_fusion.5
  881.5 4.0 convolution_bitcast_fusion.4
  885.5 4.0 convolution_bitcast_fusion.5
  893.5 4.0 convolution_bitcast_fusion.4
  897.5 4.0 convolution_bitcast_fusion.5
  909.4 4.0 convolution_bitcast_fusion.5
  921.4 4.0 convolution_bitcast_fusion.5
  933.4 4.0 convolution_bitcast_fusion.5
  945.3 4.0 convolution_bitcast_fusion.5
  957.3 4.0 convolution_bitcast_fusion.5
  969.2 4.0 convolution_bitcast_fusion.5
  981.2 4.0 convolution_bitcast_fusion.5
  993.2 4.0 convolution_bitcast_fusion.5
  1005.1 4.0 convolution_bitcast_fusion.5
  1017.1 4.0 convolution_bitcast_fusion.5
  1029.0 4.0 convolution_bitcast_fusion.5
  1041.0 4.0 convolution_bitcast_fusion.5
  1052.9 4.0 convolution_bitcast_fusion.5
  1064.9 4.0 convolution_bitcast_fusion.5
  1076.9 4.0 convolution_bitcast_fusion.5
  1088.8 4.0 convolution_bitcast_fusion.5
  1100.8 4.0 convolution_bitcast_fusion.5
  1112.7 4.0 convolution_bitcast_fusion.5
  1124.7 4.0 convolution_bitcast_fusion.5
  1136.6 4.0 convolution_bitcast_fusion.5
  1145.6 8.4 all_to_all.90
  (245 shorter events, 160.7 us)
Async XLA Ops:
  1.8 16.2 %all-to-all-start = ((s32[4,128,128]{2,0,1:T(4,128)}), s32[4,128,128]{2,0,1:T(4,128)S(1)}, u32[]{:S(2)}, u32[]{:S(2)}) async-start(s32[4,128,128]{2,0,1:T(4,128)} %copy.36), calls=%async_computation | async-start | bytes 524288 | tf_op jit(solution)/shard_map/all_to_all | solution.py:70
  270.8 6.2 copy-start
  270.8 263.6 %all-to-all-start.1 = ((bf16[64,4,128,128]{3,0,1,2:T(8,128)(2,1)}), bf16[64,4,128,128]{3,0,1,2:T(8,128)(2,1)}, u32[]{:S(2)}, u32[]{:S(2)}) async-start(bf16[64,4,128,128]{3,0,1,2:T(8,128)(2,1)} %select_bitcast_fusion.1), calls=%async_computation.1 | async-start | bytes 16777216 | tf_op jit(solution)/shard_map/all_to_all | solution.py:79
  506.4 19.2 %copy-start.1 = (s32[4,128]{1,0:T(4,128)S(1)}, s32[4,128]{1,0:T(4,128)}, u32[]{:S(2)}) copy-start(s32[4,128]{1,0:T(4,128)} %param.7) | copy-start | bytes 6148
  534.4 100.0 %all-to-all-start.3 = ((bf16[64,128,4,128]{3,2,0,1:T(4,128)(2,1)}), bf16[64,128,4,128]{3,2,0,1:T(4,128)(2,1)}, u32[]{:S(2)}, u32[]{:S(2)}) async-start(bf16[64,128,4,128]{3,2,0,1:T(4,128)(2,1)} %select_bitcast_fusion), calls=%async_computation.3 | async-start | bytes 16777216 | tf_op jit(solution)/shard_map/all_to_all | solution.py:83
  634.4 99.2 %all-to-all-start.2 = ((bf16[64,128,4,128]{3,0,2,1:T(8,128)(2,1)}), bf16[64,128,4,128]{3,0,2,1:T(8,128)(2,1)}, u32[]{:S(2)}, u32[]{:S(2)}) async-start(bf16[64,128,4,128]{3,0,2,1:T(8,128)(2,1)} %bitcast.80), calls=%async_computation.2 | async-start | bytes 16777216 | tf_op jit(solution)/shard_map/all_to_all | solution.py:82
where the time goes:
time: 1160 us
  local copies, waits for them, and re-layouts  597 us (51%)
  matrix products  259 us (22%)
  waiting for transfers between devices  143 us (12%)
  loops' own time  61.9 us (5%)
  other arithmetic  60.3 us (5%)
  starting transfers between devices  26.1 us (2%)
    gather x2, local copies, waits for them, and re-layouts, body(): own_traces = jnp.take(flat_signals, own_index, axis=1)  248 us
    gather x2, local copies, waits for them, and re-layouts, body(): remote_side = jnp.take(flat_signals, sender_index, axis=1)  245 us
    dot_general x32, matrix products, one_block(): jnp.einsum('tsrj,tk->srjk', part_a, forward, precision=lax.Precision.HIGH...  128 us
    dot_general x32, matrix products, one_block(): jnp.einsum('tsrj,tk->srjk', part_b, forward, precision=lax.Precision.HIGH...  128 us
    all_to_all x1, waiting for transfers between devices, body(): lax.all_to_all(local_side, 'tm', split_axis=1, concat_axis=0, tiled=True)  84.8 us
    another operation x1, loops' own time, predict(): spectra = lax.map(one_block, jnp.arange(blocks, dtype=jnp.int32))  61.9 us
    all_to_all x1, waiting for transfers between devices, body(): lax.all_to_all(arrived, 'tm', split_axis=1, concat_axis=0, tiled=True)  53.9 us
    unnamed x10, local copies, waits for them, and re-layouts  32.9 us
  transfers between devices with their start and end apart: 4, of which 3 were waited for; matrix products, arithmetic and copies ran while one was open for 27% of the time, Pallas kernels for 0%

commit v1 on v0

--- a/solution.py
+++ b/solution.py
@@ -3,6 +3,12 @@
 import jax.numpy as jnp
 from jax import lax
 from jax.sharding import PartitionSpec as P
+
+
+def stacked_exchange(array, mesh_axis, split, join):
+    parts = jnp.split(array, lax.axis_size(mesh_axis), axis=split)
+    incoming = lax.all_to_all(jnp.stack(parts), mesh_axis, 0, 0)
+    return jnp.concatenate(incoming, axis=join)
 
 
 def spectra_tables(length):
@@ -79,7 +85,7 @@
     arrived = lax.all_to_all(remote_side, "shot", split_axis=2, concat_axis=1, tiled=True)
     merged = convolve(
         (
-            lax.all_to_all(arrived, "tm", split_axis=1, concat_axis=0, tiled=True),
+            stacked_exchange(arrived, "tm", 1, 0),
             lax.all_to_all(local_side, "tm", split_axis=1, concat_axis=0, tiled=True),
         )
     )

time: 1160 us -> 1150 us (level)
  local copies, waits for them, and re-layouts: 597 us -> 582 us
    all_to_all x1 -> x0, local copies, waits for them, and re-layouts: 12 us -> none  [body(): lax.all_to_all(arrived, 'tm', split_axis=1, concat_axis=0, tiled=True)]
where the time goes in v1:
time: 1150 us; the launch traced here: 1140 us
  local copies, waits for them, and re-layouts  582 us (51%)
  matrix products  259 us (23%)
  waiting for transfers between devices  140 us (12%)
  other arithmetic  64.1 us (6%)
  loops' own time  61.6 us (5%)
  starting transfers between devices  26.2 us (2%)
    gather x2, local copies, waits for them, and re-layouts, body(): own_traces = jnp.take(flat_signals, own_index, axis=1)  246 us
    gather x2, local copies, waits for them, and re-layouts, body(): remote_side = jnp.take(flat_signals, sender_index, axis=1)  243 us
    dot_general x32, matrix products, one_block(): jnp.einsum('tsrj,tk->srjk', part_a, forward, precision=lax.Precision.HIGH...  128 us
    dot_general x32, matrix products, one_block(): jnp.einsum('tsrj,tk->srjk', part_b, forward, precision=lax.Precision.HIGH...  128 us
    all_to_all x1, waiting for transfers between devices, body(): lax.all_to_all(local_side, 'tm', split_axis=1, concat_axis=0, tiled=True)  81.2 us
    another operation x1, loops' own time, predict(): spectra = lax.map(one_block, jnp.arange(blocks, dtype=jnp.int32))  61.6 us
    all_to_all x1, waiting for transfers between devices, stacked_exchange(): incoming = lax.all_to_all(jnp.stack(parts), mesh_axis, 0, 0)  54 us
    unnamed x10, local copies, waits for them, and re-layouts  32.8 us
  transfers between devices with their start and end apart: 4, of which 3 were waited for; matrix products, arithmetic and copies ran while one was open for 27% of the time, Pallas kernels for 0%

profile of v1, /device:TPU:8, one launch (start us, length us, event | category | flops | bytes accessed | tf_op | source)
XLA Modules:
  0.0 1141.3 jit_solution(11945318716810012306)
XLA Ops:
  1.8 8.5 all-to-all-start
  13.3 4.8 all-to-all-done
  18.3 227.3 %gather_fusion = bf16[65536,64]{1,0:T(8,128)(2,1)} fusion(bf16[64,8192]{0,1:T(8,128)(2,1)S(1)} %bitcast.81, s32[65536]{0:T(1024)S(1)} %broadcast_clamp_fusion.1), kind=kCustom, calls=%fused_computation | custom fusion | bytes 17039360 | tf_op jit(solution)/shard_map/jit(_take)/gather | solution.py:84
  245.6 15.8 %copy.40 = bf16[4,128,128,64]{2,3,0,1:T(8,128)(2,1)} copy(bf16[4,128,128,64]{3,2,1,0:T(8,128)(2,1)} %bitcast.84) | data formatting | bytes 16777216 | tf_op jit(solution)/shard_map/jit(_take)/gather | solution.py:84
  261.6 7.6 select_bitcast_fusion.1
  269.1 6.1 all-to-all-start.1
  275.7 227.3 %gather_fusion.1 = bf16[65536,64]{1,0:T(8,128)(2,1)} fusion(bf16[64,8192]{0,1:T(8,128)(2,1)S(1)} %bitcast.82, s32[65536]{0:T(1024)S(1)} %broadcast_clamp_fusion), kind=kCustom, calls=%fused_computation.1 | custom fusion | bytes 17039360 | tf_op jit(solution)/shard_map/jit(_take)/gather | solution.py:82
  503.0 19.1 %copy.45 = bf16[128,4,128,64]{2,1,3,0:T(4,128)(2,1)} copy(bf16[128,4,128,64]{3,2,1,0:T(8,128)(2,1)} %bitcast.83) | data formatting | bytes 16777216 | tf_op jit(solution)/shard_map/jit(_take)/gather | solution.py:82
  522.5 8.5 select_bitcast_fusion
  531.0 5.7 all-to-all-start.3
  536.7 6.8 copy.41
  549.9 81.2 %all-to-all-done.3 = bf16[64,128,4,128]{3,2,0,1:T(4,128)(2,1)} async-done(((bf16[64,128,4,128]{3,2,0,1:T(4,128)(2,1)}), bf16[64,128,4,128]{3,2,0,1:T(4,128)(2,1)}, u32[]{:S(2)}, u32[]{:S(2)}) %all-to-all-start.3) | async-done | bytes 8388640 | tf_op jit(solution)/shard_map/all_to_all | solution.py:89
  631.1 5.8 all-to-all-start.2
  637.0 16.3 %copy.46 = bf16[64,128,4,128]{3,1,2,0:T(8,128)(2,1)} copy(bf16[64,128,4,128]{3,2,0,1:T(4,128)(2,1)} %all-to-all-done.3) | data formatting | bytes 16777216 | tf_op jit(solution)/shard_map/all_to_all | solution.py:89
  653.3 9.3 copy.47
  662.6 13.7 %copy.49 = bf16[256,32,4,128]{0,3,2,1:T(8,128)(2,1)} copy(bf16[256,32,4,128]{3,1,2,0:T(8,128)(2,1)} %bitcast.87) | data formatting | bytes 16777216
  676.3 54.0 %all-to-all-done.2 = bf16[4,64,32,4,128]{4,2,3,1,0:T(8,128)(2,1)} async-done(((bf16[4,64,32,4,128]{4,2,3,1,0:T(8,128)(2,1)}), bf16[4,64,32,4,128]{4,2,3,1,0:T(8,128)(2,1)}, u32[]{:S(2)}, u32[]{:S(2)}) %all-to-all-start.2) | async-done | bytes 8388640 | tf_op jit(solution)/shard_map/all_to_all | solution.py:10
  730.3 13.7 %copy.48 = bf16[256,32,4,128]{0,3,2,1:T(8,128)(2,1)} copy(bf16[256,32,4,128]{3,1,2,0:T(8,128)(2,1)} %bitcast.17) | data formatting | bytes 16777216
  744.0 382.9 %while.11 = (s32[]{:T(128)}, f32[32,1,4,512]{3,2,1,0:T(4,128)S(1)}, s32[32]{0:T(128)S(1)}, bf16[256,32,4,128]{0,3,2,1:T(8,128)(2,1)}, bf16[256,32,4,128]{0,3,2,1...) while((s32[]{:T(128)}, f32[32,1,4,512]{3,2,1,0:T(4,128)S(1)}, ...), condition=%wide.region_2.3_spmd.clone, body=%wide.region_0.0_spmd.clone.sunk | while | flops 1616637952 | bytes 8942751 | solution.py:63
  770.5 4.0 convolution_bitcast_fusion.4
  774.5 4.0 convolution_bitcast_fusion.5
  782.4 4.0 convolution_bitcast_fusion.4
  786.5 4.0 convolution_bitcast_fusion.5
  798.4 4.0 convolution_bitcast_fusion.5
  810.4 4.0 convolution_bitcast_fusion.5
  822.4 4.0 convolution_bitcast_fusion.5
  830.3 4.0 convolution_bitcast_fusion.4
  834.3 4.0 convolution_bitcast_fusion.5
  842.3 4.0 convolution_bitcast_fusion.4
  846.3 4.0 convolution_bitcast_fusion.5
  858.2 4.0 convolution_bitcast_fusion.5
  870.2 4.0 convolution_bitcast_fusion.5
  882.2 4.0 convolution_bitcast_fusion.5
  890.1 4.0 convolution_bitcast_fusion.4
  894.1 4.0 convolution_bitcast_fusion.5
  902.1 4.0 convolution_bitcast_fusion.4
  906.1 4.0 convolution_bitcast_fusion.5
  918.1 4.0 convolution_bitcast_fusion.5
  930.0 4.0 convolution_bitcast_fusion.5
  938.0 4.0 convolution_bitcast_fusion.4
  942.0 4.0 convolution_bitcast_fusion.5
  950.0 4.0 convolution_bitcast_fusion.4
  954.0 4.0 convolution_bitcast_fusion.5
  961.9 4.0 convolution_bitcast_fusion.4
  965.9 4.0 convolution_bitcast_fusion.5
  977.9 4.0 convolution_bitcast_fusion.5
  989.9 4.0 convolution_bitcast_fusion.5
  997.8 4.0 convolution_bitcast_fusion.4
  1001.8 4.0 convolution_bitcast_fusion.5
  1009.8 4.0 convolution_bitcast_fusion.4
  1013.8 4.0 convolution_bitcast_fusion.5
  1025.8 4.0 convolution_bitcast_fusion.5
  1037.7 4.0 convolution_bitcast_fusion.5
  1049.7 4.0 convolution_bitcast_fusion.5
  1057.7 4.0 convolution_bitcast_fusion.4
  1061.7 4.0 convolution_bitcast_fusion.5
  1069.6 4.0 convolution_bitcast_fusion.4
  1073.6 4.0 convolution_bitcast_fusion.5
  1085.6 4.0 convolution_bitcast_fusion.5
  1097.6 4.0 convolution_bitcast_fusion.5
  1109.5 4.0 convolution_bitcast_fusion.5
  1117.5 4.0 convolution_bitcast_fusion.4
  1121.5 4.0 convolution_bitcast_fusion.5
  1130.2 8.4 all_to_all.77
  (246 shorter events, 163.3 us)
Async XLA Ops:
  1.8 16.2 %all-to-all-start = ((s32[4,128,128]{2,0,1:T(4,128)}), s32[4,128,128]{2,0,1:T(4,128)S(1)}, u32[]{:S(2)}, u32[]{:S(2)}) async-start(s32[4,128,128]{2,0,1:T(4,128)} %copy.36), calls=%async_computation | async-start | bytes 524288 | tf_op jit(solution)/shard_map/all_to_all | solution.py:76
  269.1 6.2 copy-start
  269.1 261.9 %all-to-all-start.1 = ((bf16[64,4,128,128]{3,0,1,2:T(8,128)(2,1)}), bf16[64,4,128,128]{3,0,1,2:T(8,128)(2,1)}, u32[]{:S(2)}, u32[]{:S(2)}) async-start(bf16[64,4,128,128]{3,0,1,2:T(8,128)(2,1)} %select_bitcast_fusion.1), calls=%async_computation.1 | async-start | bytes 16777216 | tf_op jit(solution)/shard_map/all_to_all | solution.py:85
  503.0 19.2 %copy-start.1 = (s32[4,128]{1,0:T(4,128)S(1)}, s32[4,128]{1,0:T(4,128)}, u32[]{:S(2)}) copy-start(s32[4,128]{1,0:T(4,128)} %param.7) | copy-start | bytes 6148
  531.0 100.1 %all-to-all-start.3 = ((bf16[64,128,4,128]{3,2,0,1:T(4,128)(2,1)}), bf16[64,128,4,128]{3,2,0,1:T(4,128)(2,1)}, u32[]{:S(2)}, u32[]{:S(2)}) async-start(bf16[64,128,4,128]{3,2,0,1:T(4,128)(2,1)} %select_bitcast_fusion), calls=%async_computation.3 | async-start | bytes 16777216 | tf_op jit(solution)/shard_map/all_to_all | solution.py:89
  631.1 99.2 %all-to-all-start.2 = ((bf16[4,64,32,4,128]{4,2,3,1,0:T(8,128)(2,1)}), bf16[4,64,32,4,128]{4,2,3,1,0:T(8,128)(2,1)}, u32[]{:S(2)}, u32[]{:S(2)}) async-start(bf16[4,64,32,4,128]{4,2,3,1,0:T(8,128)(2,1)} %pad_maximum_fusion), calls=%async_computation.2 | async-start | bytes 16777216 | tf_op jit(solution)/shard_map/all_to_all | solution.py:10
